TPU v7x, 256 devices: a whole 4x4x8 slice. The times are simulated.
256 devices in a mesh: gx: 16 (over y_hi, x, core), gy: 16 (over y_lo, z).
Axes of the slice: x: 4, y: 4 (y_hi: 2, y_lo: 2; y = y_hi * 2 + y_lo), z: 8, core: 2. Of those that a mesh axis runs over, the one named last changes fastest.
Arguments:
- object_field: float32 [2, 8192, 8192], P(None, 'gy', 'gx'), may hold values from -6 to 6
- probe: float32 [3, 2, 256, 256], replicated, may hold values from -6 to 6
- positions: int32 [16, 16, 4, 2], P('gy', 'gx'), may hold values from 0 to 512
- frame_count: int32 [16, 16], P('gy', 'gx'), may hold values from 1 to 4, as said below
- measured: float32 [16, 16, 4, 256, 256], P('gy', 'gx'), may hold values from 0.5 to 20
Outputs:
- object_grad: float32 [2, 8192, 8192], P(None, 'gy', 'gx')
Inputs may be any that keep to these rules, and one draw needn't show every extreme that they name: `frame_count`: some tile has all 4 slots live in every draw; live frames fill the first slots of a tile; tiles in the columns tx >= 8 have exactly 1 live frame.
All inputs are finite; a program needn't handle non-finite values.
Results may differ from a plain program's by a relative error of at most 0.0045.
Values sent between devices are 32-bit elements; how exact they have to be, the bound alone decides.
A program may use at most 64 MiB of HBM per device.

v0:
```python
import math

import jax
import jax.numpy as jnp
from jax import lax
from jax.sharding import PartitionSpec as P

HALO = 128


def extended_2(array, sides, width):
    for axis, dim in sides:
        devices, length = (lax.axis_size(axis), array.shape[dim])
        up = [(i, (i + 1) % devices) for i in range(devices - 1)]
        down = [(j, i) for i, j in up]
        last = lax.slice_in_dim(array, length - width, length, axis=dim)
        initial = lax.slice_in_dim(array, 0, width, axis=dim)
        before = lax.ppermute(last, axis, up)
        after = lax.ppermute(initial, axis, down)
        array = jnp.concatenate([before, array, after], axis=dim)
    return array


def passed_along(array, axis, by):
    devices = lax.axis_size(axis)
    pairs = [(i, i + by) for i in range(devices) if 0 <= i + by < devices]
    return lax.ppermute(array, axis, pairs)


def dft_table(width, sign):
    index = jnp.arange(width, dtype=jnp.float32)
    phase = 2.0 * math.pi / width * jnp.mod(jnp.outer(index, index), width)
    scale = 1.0 / math.sqrt(width)
    cosine = jnp.cos(phase) * scale
    imag_part = sign * jnp.sin(phase) * scale
    upper = jnp.concatenate([cosine, imag_part], axis=1)
    lower = jnp.concatenate([-imag_part, cosine], axis=1)
    return jnp.concatenate([upper, lower], axis=0).astype(jnp.bfloat16)


def apply_rows(real_part, imag_part, table):
    modes, rows, width = real_part.shape
    joined = jnp.concatenate([real_part, imag_part], axis=-1).reshape(modes * rows, 2 * width)
    result = jnp.dot(joined, table, preferred_element_type=jnp.float32).reshape(
        modes, rows, 2 * width
    )
    return (result[..., :width], result[..., width:])


def frame_grad(patch, probe, measure, forward, inverse):
    probe_re = probe[:, 0]
    probe_im = probe[:, 1]
    psi_re = (probe_re * patch[0] - probe_im * patch[1]).astype(jnp.bfloat16)
    psi_im = (probe_re * patch[1] + probe_im * patch[0]).astype(jnp.bfloat16)
    half_re, half_im = apply_rows(psi_re, psi_im, forward)
    half_re = jnp.swapaxes(half_re.astype(jnp.bfloat16), 1, 2)
    half_im = jnp.swapaxes(half_im.astype(jnp.bfloat16), 1, 2)
    wave_re, wave_im = apply_rows(half_re, half_im, forward)
    inten = jnp.sum(wave_re * wave_re + wave_im * wave_im, axis=0)
    factor = 1.0 - jnp.sqrt(measure).T / jnp.sqrt(inten + 1.0)
    resid_re = (factor * wave_re).astype(jnp.bfloat16)
    resid_im = (factor * wave_im).astype(jnp.bfloat16)
    back_re, back_im = apply_rows(resid_re, resid_im, inverse)
    back_re = jnp.swapaxes(back_re.astype(jnp.bfloat16), 1, 2)
    back_im = jnp.swapaxes(back_im.astype(jnp.bfloat16), 1, 2)
    chi_re, chi_im = apply_rows(back_re, back_im, inverse)
    grad_re = jnp.sum(probe_re * chi_re + probe_im * chi_im, axis=0)
    grad_im = jnp.sum(probe_re * chi_im - probe_im * chi_re, axis=0)
    return jnp.stack([grad_re, grad_im])


def body(object_field, probe, positions, frame_count, measured):
    width = probe.shape[-1]
    border = HALO
    forward = dft_table(width, -1.0)
    inverse = dft_table(width, 1.0)
    zero = jnp.zeros((), jnp.int32)
    extended = extended_2(object_field, (("gy", 1), ("gx", 2)), border)
    spots = positions[0, 0]
    frames = measured[0, 0]
    count = frame_count[0, 0]

    def add_patch(total, grad, spot):
        old = lax.dynamic_slice(total, (zero, spot[0], spot[1]), (2, width, width))
        return lax.dynamic_update_slice(total, old + grad, (zero, spot[0], spot[1]))

    def own_frame(slot, total):
        spot = spots[slot]
        patch = lax.dynamic_slice(extended, (zero, spot[0], spot[1]), (2, width, width))
        grad = frame_grad(patch, probe, frames[slot], forward, inverse)
        return add_patch(total, grad, spot)

    start = jnp.zeros(extended.shape, jnp.float32)
    total = lax.fori_loop(0, count, own_frame, start)
    upper_rim = total[:, :border, :]
    lower_rim = total[:, -border:, :]
    from_below = passed_along(upper_rim, "gy", -1)
    from_above = passed_along(lower_rim, "gy", 1)
    middle = total[:, border:-border, :]
    middle = middle.at[:, -border:, :].add(from_below)
    middle = middle.at[:, :border, :].add(from_above)
    left_rim = middle[:, :, :border]
    right_rim = middle[:, :, -border:]
    from_right = passed_along(left_rim, "gx", -1)
    from_left = passed_along(right_rim, "gx", 1)
    inner = middle[:, :, border:-border]
    inner = inner.at[:, :, -border:].add(from_right)
    inner = inner.at[:, :, :border].add(from_left)
    return inner


def solution(mesh):
    return jax.shard_map(
        body,
        mesh=mesh,
        in_specs=(
            P(None, "gy", "gx"),
            P(),
            P("gy", "gx", None, None),
            P("gy", "gx"),
            P("gy", "gx", None, None, None),
        ),
        out_specs=P(None, "gy", "gx"),
        check_vma=False,
    )
```

profile of v0, /device:TPU:24, one launch (start us, length us, event | category | flops | bytes accessed | tf_op | source)
XLA Modules:
  0.0 185.0 jit_solution(449003033538278168)
XLA Ops:
  0.0 0.0 copy-start.2
  0.0 1.4 fusion.49
  1.4 3.8 %collective-permute-start = (f32[2,128,512]{2,1,0:T(8,128)S(1)}, f32[2,128,512]{2,1,0:T(8,128)S(1)}, u32[]{:S(2)}, u32[]{:S(2)}) collective-permute-start(f32[2,128,512]{2,1,0:T(8,128)S(1)} %get-tuple-element.150), channel_id=1, source_target_pairs={{0,1},{1,2},{2,3},{3,4},{4,5},{5,6},{6,7},{7,8},{8,9},{9,10},{10,1... | collective-permute-start | bytes 1572872 | tf_op jit(solution)/shard_map/ppermute | solution.py:18
  5.3 6.0 %collective-permute-start.1 = (f32[2,128,512]{2,1,0:T(8,128)S(1)}, f32[2,128,512]{2,1,0:T(8,128)S(1)}, u32[]{:S(2)}, u32[]{:S(2)}) collective-permute-start(f32[2,128,512]{2,1,0:T(8,128)S(1)} %get-tuple-element.149), channel_id=1, source_target_pairs={{1,0},{2,1},{3,2},{4,3},{5,4},{6,5},{7,6},{8,7},{9,8},{10,9},{11,1... | collective-permute-start | bytes 1572872 | tf_op jit(solution)/shard_map/ppermute | solution.py:19
  11.3 10.0 %collective-permute-done = f32[2,128,512]{2,1,0:T(8,128)S(1)} collective-permute-done((f32[2,128,512]{2,1,0:T(8,128)S(1)}, f32[2,128,512]{2,1,0:T(8,128)S(1)}, u32[]{:S(2)}, u32[]{:S(2)}) %collective-permute-start) | collective-permute-done | bytes 524320 | tf_op jit(solution)/shard_map/ppermute | solution.py:18
  21.3 0.0 copy-done.2
  21.3 0.2 constant_dynamic-update-slice_fusion.1
  21.5 0.0 copy-start.4
  21.5 0.9 collective-permute-done.1
  22.5 0.0 copy-start
  22.5 1.6 copy-done
  24.2 1.3 fusion.48
  25.4 1.9 %collective-permute-start.2 = (f32[2,768,128]{2,1,0:T(8,128)}, f32[2,768,128]{2,1,0:T(8,128)S(1)}, u32[]{:S(2)}, u32[]{:S(2)}) collective-permute-start(f32[2,768,128]{2,1,0:T(8,128)} %get-tuple-element.147), channel_id=1, source_target_pairs={{0,16},{16,32},{32,48},{48,64},{64,80},{80,96},{96,112},{112,128},... | collective-permute-start | bytes 2359304 | tf_op jit(solution)/shard_map/ppermute | solution.py:18
  27.4 7.3 %collective-permute-start.3 = (f32[2,768,128]{2,1,0:T(8,128)}, f32[2,768,128]{2,1,0:T(8,128)}, u32[]{:S(2)}, u32[]{:S(2)}) collective-permute-start(f32[2,768,128]{2,1,0:T(8,128)} %get-tuple-element.148), channel_id=1, source_target_pairs={{16,0},{32,16},{48,32},{64,48},{80,64},{96,80},{112,96},{128,112},... | collective-permute-start | bytes 2359304 | tf_op jit(solution)/shard_map/ppermute | solution.py:19
  34.6 0.0 copy-done.4
  34.6 0.3 copy.8
  35.0 0.0 copy-start.1
  35.0 1.7 copy.9
  36.7 1.1 fusion.44
  37.8 1.2 multiply_convert_fusion.2
  39.0 1.1 negate_convert_fusion
  40.0 1.1 fusion.33
  41.1 1.4 collective-permute-done.2
  42.6 1.9 %collective-permute-done.3 = f32[2,768,128]{2,1,0:T(8,128)} collective-permute-done((f32[2,768,128]{2,1,0:T(8,128)}, f32[2,768,128]{2,1,0:T(8,128)}, u32[]{:S(2)}, u32[]{:S(2)}) %collective-permute-start.3) | collective-permute-done | bytes 786464 | tf_op jit(solution)/shard_map/ppermute | solution.py:19
  44.4 0.0 copy-done.1
  44.4 3.7 %pad_maximum_fusion = f32[2,768,768]{2,1,0:T(8,128)} fusion(f32[2,768,128]{2,1,0:T(8,128)} %collective-permute-done.3, f32[2,768,512]{2,1,0:T(8,128)S(1)} %copy-done.1, f32[2,768,128]{2,1,0:T(8,128)S(1)} %collective-permute-done.2), kind=kLoop, calls=%fused_computation.53 | loop fusion | flops 2359296 | bytes 9437184 | tf_op jit(solution)/shard_map/concatenate | solution.py:20
  48.1 0.0 copy-start.5
  48.1 2.5 %broadcast_in_dim.2 = f32[2,768,768]{2,1,0:T(8,128)} broadcast(f32[]{:T(128)} %constant.132.clone.1), dimensions={} | broadcast | bytes 4718596 | tf_op jit(solution)/shard_map/broadcast_in_dim | solution.py:93
  50.6 0.0 copy-done.5
  50.6 23.0 %while.14 = (s32[]{:T(128)}, f32[2,768,768]{2,1,0:T(8,128)}, s32[]{:T(128)}, s32[4,2]{0,1:T(2,128)S(1)}, f32[3,2,256,256]{3,2,0,1:T(8,128)S(1)}, /*index=5*/f32[...) while((s32[]{:T(128)}, f32[2,768,768]{2,1,0:T(8,128)}, ...), condition=%wide.region_4.5_spmd, body=%wide.region_0.4_spmd.sunk | while | flops 1622671360 | bytes 28574016 | solution.py:94
  51.2 0.1 constant_dynamic-slice_fusion.2
  51.3 0.6 fusion.72
  55.9 1.3 dynamic-slice_bitcast_fusion.3
  57.3 0.2 fusion.73
  57.5 1.6 convolution_convert_fusion.4
  59.1 0.1 slice_bitcast_fusion.6
  59.2 1.6 fusion.74
  60.8 0.1 add_reduce_fusion.2
  60.9 0.1 fusion.75
  61.0 0.2 multiply_convert_fusion.4
  61.2 1.6 convolution_convert_fusion.5
  62.8 0.1 slice_bitcast_fusion.7
  62.9 1.6 fusion.76
  64.5 0.2 fusion.77
  64.8 1.4 maximum_add_fusion.2
  66.2 6.8 %dynamic_update_slice.4 = f32[2,768,768]{2,1,0:T(8,128)} dynamic-update-slice(f32[2,768,768]{2,1,0:T(8,128)} %get-tuple-element.256, f32[2,256,256]{2,1,0:T(8,128)S(1)} %maximum_add_fusion.2, s32[]{:T(128)} %constant.131.clone.1..sunk, s32[]{:T(128)S(6)} %select_n.57, s32[]{:T(128)S(6)} %select_n.58) | dynamic-update-slice | bytes 1048580 | tf_op jit(solution)/shard_map/while/body/dynamic_update_slice | solution.py:85
  73.6 1.5 fusion.46
  75.1 6.6 %collective-permute-start.4 = (f32[2,128,768]{2,1,0:T(8,128)S(1)}, f32[2,128,768]{2,1,0:T(8,128)S(1)}, u32[]{:S(2)}, u32[]{:S(2)}) collective-permute-start(f32[2,128,768]{2,1,0:T(8,128)S(1)} %get-tuple-element.144), channel_id=1, source_target_pairs={{1,0},{2,1},{3,2},{4,3},{5,4},{6,5},{7,6},{8,7},{9,8},{10,9},{11,1... | collective-permute-start | bytes 2359304 | tf_op jit(solution)/shard_map/ppermute | solution.py:27
  81.7 1.9 %collective-permute-start.5 = (f32[2,128,768]{2,1,0:T(8,128)S(1)}, f32[2,128,768]{2,1,0:T(8,128)S(1)}, u32[]{:S(2)}, u32[]{:S(2)}) collective-permute-start(f32[2,128,768]{2,1,0:T(8,128)S(1)} %get-tuple-element.143), channel_id=1, source_target_pairs={{0,1},{1,2},{2,3},{3,4},{4,5},{5,6},{6,7},{7,8},{8,9},{9,10},{10,1... | collective-permute-start | bytes 2359304 | tf_op jit(solution)/shard_map/ppermute | solution.py:27
  83.6 2.1 %slice.186 = f32[2,512,768]{2,1,0:T(8,128)S(1)} slice(f32[2,768,768]{2,1,0:T(8,128)} %get-tuple-element.101), slice={[0:2], [128:640], [0:768]} | slice | bytes 6291456 | tf_op jit(solution)/shard_map/slice | solution.py:99
  85.7 10.9 %collective-permute-done.4 = f32[2,128,768]{2,1,0:T(8,128)S(1)} collective-permute-done((f32[2,128,768]{2,1,0:T(8,128)S(1)}, f32[2,128,768]{2,1,0:T(8,128)S(1)}, u32[]{:S(2)}, u32[]{:S(2)}) %collective-permute-start.4) | collective-permute-done | bytes 786464 | tf_op jit(solution)/shard_map/ppermute | solution.py:27
  96.6 1.2 add_dynamic-update-slice_fusion
  97.8 5.0 %collective-permute-done.5 = f32[2,128,768]{2,1,0:T(8,128)S(1)} collective-permute-done((f32[2,128,768]{2,1,0:T(8,128)S(1)}, f32[2,128,768]{2,1,0:T(8,128)S(1)}, u32[]{:S(2)}, u32[]{:S(2)}) %collective-permute-start.5) | collective-permute-done | bytes 786464 | tf_op jit(solution)/shard_map/ppermute | solution.py:27
  102.8 0.2 fusion.31
  103.0 0.1 fusion.47
  103.1 65.9 %collective-permute-start.6 = (f32[2,512,128]{2,1,0:T(8,128)S(1)}, f32[2,512,128]{2,1,0:T(8,128)S(1)}, u32[]{:S(2)}, u32[]{:S(2)}) collective-permute-start(f32[2,512,128]{2,1,0:T(8,128)S(1)} %get-tuple-element.146), channel_id=1, source_target_pairs={{16,0},{32,16},{48,32},{64,48},{80,64},{96,80},{112,96},{128,112},... | collective-permute-start | bytes 1572872 | tf_op jit(solution)/shard_map/ppermute | solution.py:27
  169.0 1.9 %collective-permute-start.7 = (f32[2,512,128]{2,1,0:T(8,128)S(1)}, f32[2,512,128]{2,1,0:T(8,128)S(1)}, u32[]{:S(2)}, u32[]{:S(2)}) collective-permute-start(f32[2,512,128]{2,1,0:T(8,128)S(1)} %get-tuple-element.145), channel_id=1, source_target_pairs={{0,16},{16,32},{32,48},{48,64},{64,80},{80,96},{96,112},{112,128},... | collective-permute-start | bytes 1572872 | tf_op jit(solution)/shard_map/ppermute | solution.py:27
  171.0 0.3 slice.207
  171.2 4.5 %collective-permute-done.6 = f32[2,512,128]{2,1,0:T(8,128)S(1)} collective-permute-done((f32[2,512,128]{2,1,0:T(8,128)S(1)}, f32[2,512,128]{2,1,0:T(8,128)S(1)}, u32[]{:S(2)}, u32[]{:S(2)}) %collective-permute-start.6) | collective-permute-done | bytes 524320 | tf_op jit(solution)/shard_map/ppermute | solution.py:27
  175.7 0.1 fusion.35
  175.8 0.0 copy-start.3
  175.8 7.3 %collective-permute-done.7 = f32[2,512,128]{2,1,0:T(8,128)S(1)} collective-permute-done((f32[2,512,128]{2,1,0:T(8,128)S(1)}, f32[2,512,128]{2,1,0:T(8,128)S(1)}, u32[]{:S(2)}, u32[]{:S(2)}) %collective-permute-start.7) | collective-permute-done | bytes 524320 | tf_op jit(solution)/shard_map/ppermute | solution.py:27
  183.1 0.0 copy-done.3
  183.1 1.9 %fusion.34 = f32[2,512,512]{2,1,0:T(8,128)} fusion(f32[2,512,512]{2,1,0:T(8,128)} %copy-done.3, f32[2,512,128]{2,1,0:T(8,128)S(1)} %collective-permute-done.7), kind=kLoop, calls=%fused_computation.64 | loop fusion | flops 131072 | bytes 1572864 | tf_op jit(solution)/shard_map/scatter-add | solution.py:108
  (2 shorter events, 0.1 us)
Async XLA Ops:
  0.0 21.3 %copy-start.2 = (f32[2,512,512]{2,1,0:T(8,128)S(1)}, f32[2,512,512]{2,1,0:T(8,128)}, u32[]{:S(2)}) copy-start(f32[2,512,512]{2,1,0:T(8,128)} %param.15) | copy-start | bytes 6291460
  1.4 19.9 %collective-permute-start = (f32[2,128,512]{2,1,0:T(8,128)S(1)}, f32[2,128,512]{2,1,0:T(8,128)S(1)}, u32[]{:S(2)}, u32[]{:S(2)}) collective-permute-start(f32[2,128,512]{2,1,0:T(8,128)S(1)} %get-tuple-element.150), channel_id=1, source_target_pairs={{0,1},{1,2},{2,3},{3,4},{4,5},{5,6},{6,7},{7,8},{8,9},{9,10},{10,1... | collective-permute-start | bytes 1572872 | tf_op jit(solution)/shard_map/ppermute | solution.py:18
  5.3 17.2 %collective-permute-start.1 = (f32[2,128,512]{2,1,0:T(8,128)S(1)}, f32[2,128,512]{2,1,0:T(8,128)S(1)}, u32[]{:S(2)}, u32[]{:S(2)}) collective-permute-start(f32[2,128,512]{2,1,0:T(8,128)S(1)} %get-tuple-element.149), channel_id=1, source_target_pairs={{1,0},{2,1},{3,2},{4,3},{5,4},{6,5},{7,6},{8,7},{9,8},{10,9},{11,1... | collective-permute-start | bytes 1572872 | tf_op jit(solution)/shard_map/ppermute | solution.py:19
  21.5 13.1 %copy-start.4 = (f32[1,1,4,256,256]{4,3,2,1,0:T(8,128)S(1)}, f32[1,1,4,256,256]{4,3,2,1,0:T(8,128)}, u32[]{:S(2)}) copy-start(f32[1,1,4,256,256]{4,3,2,1,0:T(8,128)} %param.19) | copy-start | bytes 3145732
  22.5 1.7 copy-start
  25.4 17.1 %collective-permute-start.2 = (f32[2,768,128]{2,1,0:T(8,128)}, f32[2,768,128]{2,1,0:T(8,128)S(1)}, u32[]{:S(2)}, u32[]{:S(2)}) collective-permute-start(f32[2,768,128]{2,1,0:T(8,128)} %get-tuple-element.147), channel_id=1, source_target_pairs={{0,16},{16,32},{32,48},{48,64},{64,80},{80,96},{96,112},{112,128},... | collective-permute-start | bytes 2359304 | tf_op jit(solution)/shard_map/ppermute | solution.py:18
  27.4 17.1 %collective-permute-start.3 = (f32[2,768,128]{2,1,0:T(8,128)}, f32[2,768,128]{2,1,0:T(8,128)}, u32[]{:S(2)}, u32[]{:S(2)}) collective-permute-start(f32[2,768,128]{2,1,0:T(8,128)} %get-tuple-element.148), channel_id=1, source_target_pairs={{16,0},{32,16},{48,32},{64,48},{80,64},{96,80},{112,96},{128,112},... | collective-permute-start | bytes 2359304 | tf_op jit(solution)/shard_map/ppermute | solution.py:19
  35.0 9.5 %copy-start.1 = (f32[2,768,512]{2,1,0:T(8,128)S(1)}, f32[2,768,512]{2,1,0:T(8,128)}, u32[]{:S(2)}) copy-start(f32[2,768,512]{2,1,0:T(8,128)} %copy-done) | copy-start | bytes 9437188
  48.1 2.5 %copy-start.5 = (s32[1,1,4,2]{2,3,1,0:T(2,128)S(1)}, s32[1,1,4,2]{2,3,1,0:T(2,128)}, u32[]{:S(2)}) copy-start(s32[1,1,4,2]{2,3,1,0:T(2,128)} %param.17) | copy-start | bytes 100
  75.1 21.5 %collective-permute-start.4 = (f32[2,128,768]{2,1,0:T(8,128)S(1)}, f32[2,128,768]{2,1,0:T(8,128)S(1)}, u32[]{:S(2)}, u32[]{:S(2)}) collective-permute-start(f32[2,128,768]{2,1,0:T(8,128)S(1)} %get-tuple-element.144), channel_id=1, source_target_pairs={{1,0},{2,1},{3,2},{4,3},{5,4},{6,5},{7,6},{8,7},{9,8},{10,9},{11,1... | collective-permute-start | bytes 2359304 | tf_op jit(solution)/shard_map/ppermute | solution.py:27
  81.7 21.1 %collective-permute-start.5 = (f32[2,128,768]{2,1,0:T(8,128)S(1)}, f32[2,128,768]{2,1,0:T(8,128)S(1)}, u32[]{:S(2)}, u32[]{:S(2)}) collective-permute-start(f32[2,128,768]{2,1,0:T(8,128)S(1)} %get-tuple-element.143), channel_id=1, source_target_pairs={{0,1},{1,2},{2,3},{3,4},{4,5},{5,6},{6,7},{7,8},{8,9},{9,10},{10,1... | collective-permute-start | bytes 2359304 | tf_op jit(solution)/shard_map/ppermute | solution.py:27
  103.1 72.6 %collective-permute-start.6 = (f32[2,512,128]{2,1,0:T(8,128)S(1)}, f32[2,512,128]{2,1,0:T(8,128)S(1)}, u32[]{:S(2)}, u32[]{:S(2)}) collective-permute-start(f32[2,512,128]{2,1,0:T(8,128)S(1)} %get-tuple-element.146), channel_id=1, source_target_pairs={{16,0},{32,16},{48,32},{64,48},{80,64},{96,80},{112,96},{128,112},... | collective-permute-start | bytes 1572872 | tf_op jit(solution)/shard_map/ppermute | solution.py:27
  169.0 14.1 %collective-permute-start.7 = (f32[2,512,128]{2,1,0:T(8,128)S(1)}, f32[2,512,128]{2,1,0:T(8,128)S(1)}, u32[]{:S(2)}, u32[]{:S(2)}) collective-permute-start(f32[2,512,128]{2,1,0:T(8,128)S(1)} %get-tuple-element.145), channel_id=1, source_target_pairs={{0,16},{16,32},{32,48},{48,64},{64,80},{80,96},{96,112},{112,128},... | collective-permute-start | bytes 1572872 | tf_op jit(solution)/shard_map/ppermute | solution.py:27
  175.8 7.4 %copy-start.3 = (f32[2,512,512]{2,1,0:T(8,128)}, f32[2,512,512]{2,1,0:T(8,128)S(1)}, u32[]{:S(2)}) copy-start(f32[2,512,512]{2,1,0:T(8,128)S(1)} %fusion.35) | copy-start | bytes 6291460
where the time goes:
time: 188 us; the launch traced here: 185 us
  starting transfers between devices  95.4 us (51%)
  waiting for transfers between devices  41.9 us (22%)
  local copies, waits for them, and re-layouts  22 us (12%)
  other arithmetic  13.6 us (7%)
  matrix products  6.49 us (3%)
  loops' own time  5.38 us (3%)
    ppermute x4, starting transfers between devices, passed_along(): return lax.ppermute(array, axis, pairs)  76.3 us
    ppermute x4, waiting for transfers between devices, passed_along(): return lax.ppermute(array, axis, pairs)  27.7 us
    ppermute x2, starting transfers between devices, extended_2(): after = lax.ppermute(initial, axis, down)  13.3 us
    ppermute x2, waiting for transfers between devices, extended_2(): before = lax.ppermute(last, axis, up)  11.4 us
    dynamic_update_slice x1, local copies, waits for them, and re-layouts, add_patch(): return lax.dynamic_update_slice(total, old + grad, (zero, spot[0], spot[1]))  6.78 us
    dot_general x4, matrix products, apply_rows(): jnp.dot(joined, table, preferred_element_type=jnp.float32)  6.49 us
    ppermute x2, starting transfers between devices, extended_2(): before = lax.ppermute(last, axis, up)  5.73 us
    another operation x1, loops' own time, body(): total = lax.fori_loop(0, count, own_frame, start)  5.38 us
  transfers between devices with their start and end apart: 8, of which 8 were waited for; matrix products, arithmetic and copies ran while one was open for 6% of the time, Pallas kernels for 0%

commit v1 on v0

v1 whole, which is shorter than its diff:
```python
import functools
import math

import jax
import jax.numpy as jnp
import ml_dtypes
import numpy as np
from jax import lax
from jax.experimental import pallas as pl
from jax.experimental.pallas import tpu as pltpu
from jax.sharding import PartitionSpec as P

HALO = 128
W = 256
H = 128
LANES = 128
F32 = jnp.float32
BF16 = jnp.bfloat16


def dft_tables():
    j = np.arange(H)[:, None]
    k = np.arange(H)[None, :]
    tables = []
    for odd in (0, 1):
        phase = 2.0 * math.pi / W * np.mod(j * (2 * k + odd), W)
        cosine = np.cos(phase) / math.sqrt(W)
        sine = np.sin(phase) / math.sqrt(W)
        tables.append(np.block([[cosine, -sine], [sine, cosine]]))
    tables += [tables[0].T, tables[1].T]
    return np.stack(tables).astype(ml_dtypes.bfloat16)


def dot(a, b):
    return jnp.dot(a, b, preferred_element_type=F32)


def frames_kernel(
    spots, count, tables, probe, root, own, above, below, before, after,
    total_out,
    ext, total, patch, stage2, wave, stage3, stage4, grad, sem,
):
    modes = probe.shape[0]
    tile = own.shape[1]
    side = tile + 2 * HALO
    copies = []

    def load(source, rows, first):
        for i in range(source.shape[2] // LANES):
            n = len(copies)
            copy = pltpu.make_async_copy(source.at[:, :, pl.ds(i * LANES, LANES)], ext.at[:, first + i, rows, :], sem.at[n])
            copy.start()
            copies.append(copy)

    load(own, pl.ds(HALO, tile), 1)
    load(above, pl.ds(0, HALO), 1)
    load(below, pl.ds(HALO + tile, HALO), 1)
    load(before, pl.ds(0, side), 0)
    load(after, pl.ds(0, side), 1 + tile // LANES)

    @pl.loop(0, side // 16)
    def _(i):
        total[:, :, pl.ds(pl.multiple_of(i * 16, 16), 16), :] = jnp.zeros((2, total.shape[1], 16, LANES), F32)

    for copy in copies:
        copy.wait()

    lane = lax.broadcasted_iota(jnp.int32, (W, LANES), 1)

    @pl.loop(0, count[0, 0])
    def _(slot):
        row = spots[slot, 0]
        column = spots[slot, 1]
        block = column // LANES
        shift = column - block * LANES
        back = lax.rem(LANES - shift, LANES)
        keep = lane < LANES - shift
        for part in range(2):
            rolled = []
            for i in range(3):
                x = ext[part, block + i, pl.ds(row, W), :]
                rolled.append(pltpu.roll(x, back, axis=1))
            for i in range(2):
                patch[part, :, i * LANES:(i + 1) * LANES] = jnp.where(keep, rolled[i], rolled[i + 1])

        step = 32
        @pl.loop(0, H // step)
        def _(i):
            first = pl.multiple_of(i * step, step)
            even, odd = [], []
            for m in range(modes):
                for half in range(2):
                    rows = pl.ds(half * H + first, step)
                    pr, pi = probe[m, 0, rows, :], probe[m, 1, rows, :]
                    xr, xi = patch[0, rows, :], patch[1, rows, :]
                    re = pr * xr - pi * xi
                    im = pr * xi + pi * xr
                    even.append(jnp.concatenate([re[:, :H] + re[:, H:], im[:, :H] + im[:, H:]], axis=1))
                    odd.append(jnp.concatenate([re[:, :H] - re[:, H:], im[:, :H] - im[:, H:]], axis=1))
            even = dot(jnp.concatenate(even, axis=0).astype(BF16), tables[0])
            odd = dot(jnp.concatenate(odd, axis=0).astype(BF16), tables[1])
            for m in range(modes):
                for n, h in enumerate((even, odd)):
                    low = h[(2 * m) * step:(2 * m + 1) * step]
                    high = h[(2 * m + 1) * step:(2 * m + 2) * step]
                    plus, minus = (low + high).astype(BF16), (low - high).astype(BF16)
                    for part in range(2):
                        rows = pl.ds(part * H + first, step)
                        columns = slice(part * H, (part + 1) * H)
                        stage2[m, 0, rows, n * H:(n + 1) * H] = plus[:, columns]
                        stage2[m, 1, rows, n * H:(n + 1) * H] = minus[:, columns]

        for m in range(modes):
            for n in range(2):
                wave[m, n] = dot(tables[2 + n], stage2[m, n])

        for n in range(2):
            @pl.loop(0, H // 16)
            def _(i):
                first = pl.multiple_of(i * 16, 16)
                res = [wave[m, n, pl.ds(first, 16), :] for m in range(modes)]
                ims = [wave[m, n, pl.ds(H + first, 16), :] for m in range(modes)]
                inten = sum(x * x for x in res) + sum(x * x for x in ims)
                factor = 1.0 - root[slot, pl.ds(n * H + first, 16), :] / jnp.sqrt(inten + 1.0)
                for m in range(modes):
                    stage3[m, n, pl.ds(first, 16), :] = (factor * res[m]).astype(BF16)
                    stage3[m, n, pl.ds(H + first, 16), :] = (factor * ims[m]).astype(BF16)

        for m in range(modes):
            even = dot(tables[0], stage3[m, 0])
            odd = dot(tables[1], stage3[m, 1])
            plus, minus = (even + odd).astype(BF16), (even - odd).astype(BF16)
            for half, x in enumerate((plus, minus)):
                for part in range(2):
                    for n in range(2):
                        stage4[n, m, half * H:(half + 1) * H, part * H:(part + 1) * H] = x[part * H:(part + 1) * H, n * H:(n + 1) * H]

        @pl.loop(0, W // step)
        def _(i):
            rows = pl.ds(pl.multiple_of(i * step, step), step)
            even = dot(stage4[0, :, rows, :].reshape(modes * step, W), tables[2])
            odd = dot(stage4[1, :, rows, :].reshape(modes * step, W), tables[3])
            plus, minus = even + odd, even - odd
            for half, x in enumerate((plus, minus)):
                columns = slice(half * H, (half + 1) * H)
                gr = gi = 0.0
                for m in range(modes):
                    pr, pi = probe[m, 0, rows, columns], probe[m, 1, rows, columns]
                    cr, ci = x[m * step:(m + 1) * step, :H], x[m * step:(m + 1) * step, H:]
                    gr = gr + (pr * cr + pi * ci)
                    gi = gi + (pr * ci - pi * cr)
                grad[0, rows, columns] = gr
                grad[1, rows, columns] = gi

        moved = lane >= shift
        for part in range(2):
            left = pltpu.roll(grad[part, :, 0:LANES], shift, axis=1)
            right = pltpu.roll(grad[part, :, LANES:2 * LANES], shift, axis=1)
            zero = jnp.zeros_like(left)
            pieces = (jnp.where(moved, left, zero), jnp.where(moved, right, left), jnp.where(moved, zero, right))
            for i, piece in enumerate(pieces):
                where = (part, block + i, pl.ds(row, W), slice(None))
                total[where] = total[where] + piece

    copies = [
        pltpu.make_async_copy(total.at[:, i], total_out.at[:, :, pl.ds(i * LANES, LANES)], sem.at[i])
        for i in range(side // LANES)
    ]
    for copy in copies:
        copy.start()
    for copy in copies:
        copy.wait()


def frames_call(spots, count, probe, root, own, above, below, before, after):
    modes = probe.shape[0]
    side = own.shape[1] + 2 * HALO
    wide = side + LANES
    smem = pl.BlockSpec(memory_space=pltpu.SMEM)
    vmem = pl.BlockSpec(memory_space=pltpu.VMEM)
    hbm = pl.BlockSpec(memory_space=pl.ANY)
    return pl.pallas_call(
        frames_kernel,
        out_shape=jax.ShapeDtypeStruct((2, side, side), F32),
        in_specs=[smem, smem, vmem, vmem, vmem, hbm, hbm, hbm, hbm, hbm],
        out_specs=hbm,
        scratch_shapes=[
            pltpu.VMEM((2, wide // LANES, side, LANES), F32),
            pltpu.VMEM((2, wide // LANES, side, LANES), F32),
            pltpu.VMEM((2, W, W), F32),
            pltpu.VMEM((modes, 2, W, W), BF16),
            pltpu.VMEM((modes, 2, W, W), F32),
            pltpu.VMEM((modes, 2, W, W), BF16),
            pltpu.VMEM((2, modes, W, W), BF16),
            pltpu.VMEM((2, W, W), F32),
            pltpu.SemaphoreType.DMA((16,)),
        ],
        compiler_params=pltpu.CompilerParams(vmem_limit_bytes=60 * 1024 * 1024),
        name="frames",
    )(spots, count, jnp.asarray(dft_tables()), probe, root, own, above, below, before, after)


def passed_along(array, axis, by):
    devices = lax.axis_size(axis)
    pairs = [(i, i + by) for i in range(devices) if 0 <= i + by < devices]
    return lax.ppermute(array, axis, pairs)


def body(object_field, probe, positions, frame_count, measured):
    border = HALO
    spots = positions[0, 0]
    count = frame_count
    root = jnp.sqrt(measured[0, 0])
    slots = root.shape[0]
    root = root.reshape(slots, H, 2, H, 2).transpose(0, 2, 1, 4, 3).reshape(slots, W, W)
    above = passed_along(object_field[:, -border:, :], "gy", 1)
    below = passed_along(object_field[:, :border, :], "gy", -1)
    left = jnp.concatenate([x[:, :, :border] for x in (above, object_field, below)], axis=1)
    right = jnp.concatenate([x[:, :, -border:] for x in (above, object_field, below)], axis=1)
    before = passed_along(right, "gx", 1)
    after = passed_along(left, "gx", -1)

    total = frames_call(spots, count, probe, root, object_field, above, below, before, after)

    upper_rim = total[:, :border, :]
    lower_rim = total[:, -border:, :]
    from_below = passed_along(upper_rim, "gy", -1)
    from_above = passed_along(lower_rim, "gy", 1)
    middle = total[:, border:-border, :]
    middle = middle.at[:, -border:, :].add(from_below)
    middle = middle.at[:, :border, :].add(from_above)
    left_rim = middle[:, :, :border]
    right_rim = middle[:, :, -border:]
    from_right = passed_along(left_rim, "gx", -1)
    from_left = passed_along(right_rim, "gx", 1)
    inner = middle[:, :, border:-border]
    inner = inner.at[:, :, -border:].add(from_right)
    inner = inner.at[:, :, :border].add(from_left)
    return inner


def solution(mesh):
    return jax.shard_map(
        body,
        mesh=mesh,
        in_specs=(
            P(None, "gy", "gx"),
            P(),
            P("gy", "gx", None, None),
            P("gy", "gx"),
            P("gy", "gx", None, None, None),
        ),
        out_specs=P(None, "gy", "gx"),
        check_vma=False,
    )
```

time: 188 us -> 164 us (0.87)
  starting transfers between devices: 95.4 us -> 45.3 us
  local copies, waits for them, and re-layouts: 22 us -> 60.1 us
  Pallas kernels: 0 us -> 10.8 us
  other arithmetic: 13.6 us -> 4.23 us
  matrix products: 6.49 us -> 0 us
  loops' own time: 5.38 us -> 0 us
    transpose x2 -> x1, local copies, waits for them, and re-layouts: 0.11 us -> 36.1 us  [body(): root.reshape(slots, H, 2, H, 2).transpose(0, 2, 1, 4, 3)]
    ppermute x4 -> x8, starting transfers between devices: 76.3 us -> 45.3 us  [passed_along(): return lax.ppermute(array, axis, pairs)]
    ppermute x4 -> x0, starting transfers between devices: 19 us -> none  [the longest x2 13.3 us: extended_2(): after = lax.ppermute(initial, axis, down)]
    sqrt x0 -> x2, local copies, waits for them, and re-layouts: none -> 16.8 us  [body(): root = jnp.sqrt(measured[0, 0])]
    ppermute x4 -> x0, waiting for transfers between devices: 14.2 us -> none  [the longest x2 11.4 us: extended_2(): before = lax.ppermute(last, axis, up)]
    ppermute x4 -> x8, waiting for transfers between devices: 27.7 us -> 41.6 us  [passed_along(): return lax.ppermute(array, axis, pairs)]
    pallas_call x0 -> x1, Pallas kernels: none -> 10.8 us  [frames_call(): pl.pallas_call(frames_kernel, out_shape=jax.ShapeDtypeStruct((2, side, si...]
    dynamic_update_slice x1 -> x0, local copies, waits for them, and re-layouts: 6.78 us -> none  [add_patch(): return lax.dynamic_update_slice(total, old + grad, (zero, spot[0], spot[1]))]
  transfers between devices with their start and end apart: 8 -> 8, of which waited for: 8 -> 6; matrix products, arithmetic and copies ran while one was open for 6% -> 36% of each run, Pallas kernels for 0% -> 0%
where the time goes in v1:
time: 164 us; the launch traced here: 163 us
  local copies, waits for them, and re-layouts  60.1 us (37%)
  starting transfers between devices  45.3 us (28%)
  waiting for transfers between devices  41.6 us (25%)
  Pallas kernels  10.8 us (7%)
  other arithmetic  4.23 us (3%)
    ppermute x8, starting transfers between devices, passed_along(): return lax.ppermute(array, axis, pairs)  45.3 us
    ppermute x8, waiting for transfers between devices, passed_along(): return lax.ppermute(array, axis, pairs)  41.6 us
    transpose x1, local copies, waits for them, and re-layouts, body(): root.reshape(slots, H, 2, H, 2).transpose(0, 2, 1, 4, 3)  36.1 us
    sqrt x2, local copies, waits for them, and re-layouts, body(): root = jnp.sqrt(measured[0, 0])  16.8 us
    pallas_call x1, Pallas kernels, frames_call(): pl.pallas_call(frames_kernel, out_shape=jax.ShapeDtypeStruct((2, side, si...  10.8 us
  transfers between devices with their start and end apart: 8, of which 6 were waited for; matrix products, arithmetic and copies ran while one was open for 36% of the time, Pallas kernels for 0%

profile of v1, /device:TPU:24, one launch (start us, length us, event | category | flops | bytes accessed | tf_op | source)
XLA Modules:
  0.0 162.8 jit_solution(1709899402629477801)
XLA Ops:
  0.0 1.3 fusion.7
  1.3 7.9 %collective-permute-start.1 = (f32[2,128,512]{2,1,0:T(8,128)S(1)}, f32[2,128,512]{2,1,0:T(8,128)S(1)}, u32[]{:S(2)}, u32[]{:S(2)}) collective-permute-start(f32[2,128,512]{2,1,0:T(8,128)S(1)} %get-tuple-element.59), channel_id=1, source_target_pairs={{1,0},{2,1},{3,2},{4,3},{5,4},{6,5},{7,6},{8,7},{9,8},{10,9},{11,1... | collective-permute-start | bytes 1572872 | tf_op jit(solution)/shard_map/ppermute | solution.py:206
  9.2 0.0 copy-start.5
  9.2 0.0 copy-start.4
  9.2 2.1 %collective-permute-start = (f32[2,128,512]{2,1,0:T(8,128)S(1)}, f32[2,128,512]{2,1,0:T(8,128)S(1)}, u32[]{:S(2)}, u32[]{:S(2)}) collective-permute-start(f32[2,128,512]{2,1,0:T(8,128)S(1)} %get-tuple-element.60), channel_id=1, source_target_pairs={{0,1},{1,2},{2,3},{3,4},{4,5},{5,6},{6,7},{7,8},{8,9},{9,10},{10,1... | collective-permute-start | bytes 1572872 | tf_op jit(solution)/shard_map/ppermute | solution.py:206
  11.3 1.3 fusion.6
  12.6 7.8 %collective-permute-done.1.below = f32[2,128,512]{2,1,0:T(8,128)S(1)} collective-permute-done((f32[2,128,512]{2,1,0:T(8,128)S(1)}, f32[2,128,512]{2,1,0:T(8,128)S(1)}, u32[]{:S(2)}, u32[]{:S(2)}) %collective-permute-start.1) | collective-permute-done | bytes 524320 | tf_op jit(solution)/shard_map/ppermute | solution.py:206
  20.4 0.0 copy-start.2
  20.4 6.4 %collective-permute-done.above = f32[2,128,512]{2,1,0:T(8,128)S(1)} collective-permute-done((f32[2,128,512]{2,1,0:T(8,128)S(1)}, f32[2,128,512]{2,1,0:T(8,128)S(1)}, u32[]{:S(2)}, u32[]{:S(2)}) %collective-permute-start) | collective-permute-done | bytes 524320 | tf_op jit(solution)/shard_map/ppermute | solution.py:206
  26.8 0.0 copy-start.3
  26.8 1.0 pad_maximum_fusion
  27.8 1.9 %collective-permute-start.2 = (f32[2,768,128]{2,1,0:T(8,128)}, f32[2,768,128]{2,1,0:T(8,128)}, u32[]{:S(2)}, u32[]{:S(2)}) collective-permute-start(f32[2,768,128]{2,1,0:T(8,128)} %pad_maximum_fusion), channel_id=1, source_target_pairs={{0,16},{16,32},{32,48},{48,64},{64,80},{80,96},{96,112},{112,128},... | collective-permute-start | bytes 2359304 | tf_op jit(solution)/shard_map/ppermute | solution.py:206
  29.7 0.9 pad_maximum_fusion.1
  30.7 7.2 %collective-permute-start.3 = (f32[2,768,128]{2,1,0:T(8,128)}, f32[2,768,128]{2,1,0:T(8,128)}, u32[]{:S(2)}, u32[]{:S(2)}) collective-permute-start(f32[2,768,128]{2,1,0:T(8,128)} %pad_maximum_fusion.1), channel_id=1, source_target_pairs={{16,0},{32,16},{48,32},{64,48},{80,64},{96,80},{112,96},{128,112},... | collective-permute-start | bytes 2359304 | tf_op jit(solution)/shard_map/ppermute | solution.py:206
  37.9 0.0 copy-done.5
  37.9 0.7 copy.11.spots
  39.3 0.0 copy-done.4
  39.3 0.2 sqrt.7
  39.5 0.0 copy-done.2
  39.5 16.6 %copy.9 = f32[1,1,4,256,256]{2,4,3,1,0:T(8,128)} copy(f32[1,1,4,256,256]{4,3,2,1,0:T(8,128)S(1)} %sqrt.7) | data formatting | bytes 2097152 | tf_op jit(solution)/shard_map/sqrt | solution.py:213
  56.1 0.0 copy-done.3
  56.1 36.1 %copy.10 = f32[4,2,128,2,128]{4,3,2,1,0:T(2,128)S(1)} copy(f32[4,2,128,2,128]{0,3,4,1,2:T(2,128)} %bitcast.4) | data formatting | bytes 2097152 | tf_op jit(solution)/shard_map/transpose | solution.py:215
  92.3 1.8 %reshape.123.root = f32[4,256,256]{2,1,0:T(8,128)} reshape(f32[4,2,128,2,128]{4,3,2,1,0:T(2,128)S(1)} %copy.10) | data formatting | bytes 2097152 | tf_op jit(solution)/shard_map/reshape | solution.py:215
  94.1 0.0 collective-permute-done.2.before
  94.1 0.0 collective-permute-done.3.after
  94.1 10.8 %frames.1 = f32[2,768,768]{2,1,0:T(8,128)} custom-call(s32[4,2]{1,0:T(4,128)} %copy.11.spots, s32[1,1]{1,0:T(1,128)S(6)} %copy.16.count, bf16[4,256,256]{2,1,0:T(8,128)(2,1)} %constant.108.clone.tables, f32[3,2,256,256]{3,2,1,0:T(8,128)} %probe.1, f32[4,256,256]{2,1,0:T(8,128)} %reshape.123.root, f32[2,512,512]{2,1,0:T(8,128)} %own.1, ...), custom_call_target="tpu_custom_call" | custom-call | tf_op jit(solution)/shard_map/frames/pallas_call | solution.py:182
  104.8 0.0 copy-start
  104.9 1.7 %fusion.4 = (f32[2,128,768]{2,1,0:T(8,128)S(1)}, f32[2,128,768]{2,1,0:T(8,128)S(1)}) fusion(f32[2,768,768]{2,1,0:T(8,128)} %frames.1), kind=kLoop, calls=%fused_computation.10 | loop fusion | bytes 3145728 | tf_op jit(solution)/shard_map/slice | solution.py:226
  106.5 2.1 %collective-permute-start.4 = (f32[2,128,768]{2,1,0:T(8,128)S(1)}, f32[2,128,768]{2,1,0:T(8,128)S(1)}, u32[]{:S(2)}, u32[]{:S(2)}) collective-permute-start(f32[2,128,768]{2,1,0:T(8,128)S(1)} %get-tuple-element.54), channel_id=1, source_target_pairs={{1,0},{2,1},{3,2},{4,3},{5,4},{6,5},{7,6},{8,7},{9,8},{10,9},{11,1... | collective-permute-start | bytes 2359304 | tf_op jit(solution)/shard_map/ppermute | solution.py:206
  108.6 0.0 slice-start
  108.6 4.2 %collective-permute-start.5 = (f32[2,128,768]{2,1,0:T(8,128)S(1)}, f32[2,128,768]{2,1,0:T(8,128)S(1)}, u32[]{:S(2)}, u32[]{:S(2)}) collective-permute-start(f32[2,128,768]{2,1,0:T(8,128)S(1)} %get-tuple-element.53), channel_id=1, source_target_pairs={{0,1},{1,2},{2,3},{3,4},{4,5},{5,6},{6,7},{7,8},{8,9},{9,10},{10,1... | collective-permute-start | bytes 2359304 | tf_op jit(solution)/shard_map/ppermute | solution.py:206
  112.8 11.5 %collective-permute-done.4 = f32[2,128,768]{2,1,0:T(8,128)S(1)} collective-permute-done((f32[2,128,768]{2,1,0:T(8,128)S(1)}, f32[2,128,768]{2,1,0:T(8,128)S(1)}, u32[]{:S(2)}, u32[]{:S(2)}) %collective-permute-start.4) | collective-permute-done | bytes 786464 | tf_op jit(solution)/shard_map/ppermute | solution.py:206
  124.2 0.0 copy-done
  124.2 0.0 slice-done
  124.2 0.1 fusion.1
  124.3 4.2 %collective-permute-done.5 = f32[2,128,768]{2,1,0:T(8,128)S(1)} collective-permute-done((f32[2,128,768]{2,1,0:T(8,128)S(1)}, f32[2,128,768]{2,1,0:T(8,128)S(1)}, u32[]{:S(2)}, u32[]{:S(2)}) %collective-permute-start.5) | collective-permute-done | bytes 786464 | tf_op jit(solution)/shard_map/ppermute | solution.py:206
  128.5 0.2 fusion
  128.7 0.1 fusion.5
  128.8 17.9 %collective-permute-start.6 = (f32[2,512,128]{2,1,0:T(8,128)S(1)}, f32[2,512,128]{2,1,0:T(8,128)S(1)}, u32[]{:S(2)}, u32[]{:S(2)}) collective-permute-start(f32[2,512,128]{2,1,0:T(8,128)S(1)} %get-tuple-element.56), channel_id=1, source_target_pairs={{16,0},{32,16},{48,32},{64,48},{80,64},{96,80},{112,96},{128,112},... | collective-permute-start | bytes 1572872 | tf_op jit(solution)/shard_map/ppermute | solution.py:206
  146.8 1.9 %collective-permute-start.7 = (f32[2,512,128]{2,1,0:T(8,128)S(1)}, f32[2,512,128]{2,1,0:T(8,128)S(1)}, u32[]{:S(2)}, u32[]{:S(2)}) collective-permute-start(f32[2,512,128]{2,1,0:T(8,128)S(1)} %get-tuple-element.55), channel_id=1, source_target_pairs={{0,16},{16,32},{32,48},{48,64},{64,80},{80,96},{96,112},{112,128},... | collective-permute-start | bytes 1572872 | tf_op jit(solution)/shard_map/ppermute | solution.py:206
  148.7 0.3 slice.167
  149.0 4.4 %collective-permute-done.6 = f32[2,512,128]{2,1,0:T(8,128)S(1)} collective-permute-done((f32[2,512,128]{2,1,0:T(8,128)S(1)}, f32[2,512,128]{2,1,0:T(8,128)S(1)}, u32[]{:S(2)}, u32[]{:S(2)}) %collective-permute-start.6) | collective-permute-done | bytes 524320 | tf_op jit(solution)/shard_map/ppermute | solution.py:206
  153.4 0.1 fusion.3
  153.5 0.0 copy-start.1
  153.5 7.3 %collective-permute-done.7 = f32[2,512,128]{2,1,0:T(8,128)S(1)} collective-permute-done((f32[2,512,128]{2,1,0:T(8,128)S(1)}, f32[2,512,128]{2,1,0:T(8,128)S(1)}, u32[]{:S(2)}, u32[]{:S(2)}) %collective-permute-start.7) | collective-permute-done | bytes 524320 | tf_op jit(solution)/shard_map/ppermute | solution.py:206
  160.9 0.0 copy-done.1
  160.9 1.9 %fusion.2 = f32[2,512,512]{2,1,0:T(8,128)} fusion(f32[2,512,512]{2,1,0:T(8,128)} %copy-done.1, f32[2,512,128]{2,1,0:T(8,128)S(1)} %collective-permute-done.7), kind=kLoop, calls=%fused_computation.7 | loop fusion | flops 131072 | bytes 1572864 | tf_op jit(solution)/shard_map/scatter-add | solution.py:238
  (2 shorter events, 0.0 us)
Async XLA Ops:
  1.3 19.1 %collective-permute-start.1 = (f32[2,128,512]{2,1,0:T(8,128)S(1)}, f32[2,128,512]{2,1,0:T(8,128)S(1)}, u32[]{:S(2)}, u32[]{:S(2)}) collective-permute-start(f32[2,128,512]{2,1,0:T(8,128)S(1)} %get-tuple-element.59), channel_id=1, source_target_pairs={{1,0},{2,1},{3,2},{4,3},{5,4},{6,5},{7,6},{8,7},{9,8},{10,9},{11,1... | collective-permute-start | bytes 1572872 | tf_op jit(solution)/shard_map/ppermute | solution.py:206
  9.2 28.7 %copy-start.5 = (s32[1,1,4,2]{2,3,1,0:T(2,128)S(1)}, s32[1,1,4,2]{2,3,1,0:T(2,128)}, u32[]{:S(2)}) copy-start(s32[1,1,4,2]{2,3,1,0:T(2,128)} %param.16) | copy-start | bytes 100
  9.2 30.0 %copy-start.4 = (f32[1,1,4,256,256]{4,3,2,1,0:T(8,128)S(1)}, f32[1,1,4,256,256]{4,3,2,1,0:T(8,128)}, u32[]{:S(2)}) copy-start(f32[1,1,4,256,256]{4,3,2,1,0:T(8,128)} %param.18) | copy-start | bytes 3145732
  9.2 17.5 %collective-permute-start = (f32[2,128,512]{2,1,0:T(8,128)S(1)}, f32[2,128,512]{2,1,0:T(8,128)S(1)}, u32[]{:S(2)}, u32[]{:S(2)}) collective-permute-start(f32[2,128,512]{2,1,0:T(8,128)S(1)} %get-tuple-element.60), channel_id=1, source_target_pairs={{0,1},{1,2},{2,3},{3,4},{4,5},{5,6},{6,7},{7,8},{8,9},{9,10},{10,1... | collective-permute-start | bytes 1572872 | tf_op jit(solution)/shard_map/ppermute | solution.py:206
  20.4 19.2 %copy-start.2 = (f32[2,128,512]{2,1,0:T(8,128)}, f32[2,128,512]{2,1,0:T(8,128)S(1)}, u32[]{:S(2)}) copy-start(f32[2,128,512]{2,1,0:T(8,128)S(1)} %collective-permute-done.1.below) | copy-start | bytes 1572868
  26.8 29.3 %copy-start.3 = (f32[2,128,512]{2,1,0:T(8,128)}, f32[2,128,512]{2,1,0:T(8,128)S(1)}, u32[]{:S(2)}) copy-start(f32[2,128,512]{2,1,0:T(8,128)S(1)} %collective-permute-done.above) | copy-start | bytes 1572868
  27.8 66.2 %collective-permute-start.2 = (f32[2,768,128]{2,1,0:T(8,128)}, f32[2,768,128]{2,1,0:T(8,128)}, u32[]{:S(2)}, u32[]{:S(2)}) collective-permute-start(f32[2,768,128]{2,1,0:T(8,128)} %pad_maximum_fusion), channel_id=1, source_target_pairs={{0,16},{16,32},{32,48},{48,64},{64,80},{80,96},{96,112},{112,128},... | collective-permute-start | bytes 2359304 | tf_op jit(solution)/shard_map/ppermute | solution.py:206
  30.7 63.4 %collective-permute-start.3 = (f32[2,768,128]{2,1,0:T(8,128)}, f32[2,768,128]{2,1,0:T(8,128)}, u32[]{:S(2)}, u32[]{:S(2)}) collective-permute-start(f32[2,768,128]{2,1,0:T(8,128)} %pad_maximum_fusion.1), channel_id=1, source_target_pairs={{16,0},{32,16},{48,32},{64,48},{80,64},{96,80},{112,96},{128,112},... | collective-permute-start | bytes 2359304 | tf_op jit(solution)/shard_map/ppermute | solution.py:206
  104.8 19.4 %copy-start = (f32[2,768,768]{2,1,0:T(8,128)S(1)}, f32[2,768,768]{2,1,0:T(8,128)}, u32[]{:S(2)}) copy-start(f32[2,768,768]{2,1,0:T(8,128)} %frames.1) | copy-start | bytes 14155780
  106.5 17.7 %collective-permute-start.4 = (f32[2,128,768]{2,1,0:T(8,128)S(1)}, f32[2,128,768]{2,1,0:T(8,128)S(1)}, u32[]{:S(2)}, u32[]{:S(2)}) collective-permute-start(f32[2,128,768]{2,1,0:T(8,128)S(1)} %get-tuple-element.54), channel_id=1, source_target_pairs={{1,0},{2,1},{3,2},{4,3},{5,4},{6,5},{7,6},{8,7},{9,8},{10,9},{11,1... | collective-permute-start | bytes 2359304 | tf_op jit(solution)/shard_map/ppermute | solution.py:206
  108.6 15.7 %slice-start = ((f32[2,768,768]{2,1,0:T(8,128)}), f32[2,512,768]{2,1,0:T(8,128)S(1)}, s32[]{:S(2)}) async-start(f32[2,768,768]{2,1,0:T(8,128)} %frames.1), calls=%async_computation | async-start | bytes 6291456 | tf_op jit(solution)/shard_map/slice | solution.py:229
  108.6 20.0 %collective-permute-start.5 = (f32[2,128,768]{2,1,0:T(8,128)S(1)}, f32[2,128,768]{2,1,0:T(8,128)S(1)}, u32[]{:S(2)}, u32[]{:S(2)}) collective-permute-start(f32[2,128,768]{2,1,0:T(8,128)S(1)} %get-tuple-element.53), channel_id=1, source_target_pairs={{0,1},{1,2},{2,3},{3,4},{4,5},{5,6},{6,7},{7,8},{8,9},{9,10},{10,1... | collective-permute-start | bytes 2359304 | tf_op jit(solution)/shard_map/ppermute | solution.py:206
  128.8 24.6 %collective-permute-start.6 = (f32[2,512,128]{2,1,0:T(8,128)S(1)}, f32[2,512,128]{2,1,0:T(8,128)S(1)}, u32[]{:S(2)}, u32[]{:S(2)}) collective-permute-start(f32[2,512,128]{2,1,0:T(8,128)S(1)} %get-tuple-element.56), channel_id=1, source_target_pairs={{16,0},{32,16},{48,32},{64,48},{80,64},{96,80},{112,96},{128,112},... | collective-permute-start | bytes 1572872 | tf_op jit(solution)/shard_map/ppermute | solution.py:206
  146.8 14.1 %collective-permute-start.7 = (f32[2,512,128]{2,1,0:T(8,128)S(1)}, f32[2,512,128]{2,1,0:T(8,128)S(1)}, u32[]{:S(2)}, u32[]{:S(2)}) collective-permute-start(f32[2,512,128]{2,1,0:T(8,128)S(1)} %get-tuple-element.55), channel_id=1, source_target_pairs={{0,16},{16,32},{32,48},{48,64},{64,80},{80,96},{96,112},{112,128},... | collective-permute-start | bytes 1572872 | tf_op jit(solution)/shard_map/ppermute | solution.py:206
  153.5 7.3 %copy-start.1 = (f32[2,512,512]{2,1,0:T(8,128)}, f32[2,512,512]{2,1,0:T(8,128)S(1)}, u32[]{:S(2)}) copy-start(f32[2,512,512]{2,1,0:T(8,128)S(1)} %fusion.3) | copy-start | bytes 6291460

commit v2 on v1

--- a/solution.py
+++ b/solution.py
@@ -16,6 +16,7 @@
 LANES = 128
 F32 = jnp.float32
 BF16 = jnp.bfloat16
+MESH = pl.DeviceIdType.MESH
 
 
 def dft_tables():
@@ -35,35 +36,310 @@
     return jnp.dot(a, b, preferred_element_type=F32)
 
 
+def neighbours(mesh_shape):
+    ny, nx = mesh_shape
+    y, x = lax.axis_index("gy"), lax.axis_index("gx")
+    return y, x, dict(up=y > 0, down=y < ny - 1, left=x > 0, right=x < nx - 1)
+
+
+def device(direction, y, x, mesh_shape):
+    ny, nx = mesh_shape
+    return {
+        "up": (jnp.maximum(y - 1, 0), x),
+        "down": (jnp.minimum(y + 1, ny - 1), x),
+        "left": (y, jnp.maximum(x - 1, 0)),
+        "right": (y, jnp.minimum(x + 1, nx - 1)),
+    }[direction]
+
+
+OPPOSITE = dict(up="down", down="up", left="right", right="left")
+
+
+class Exchange:
+    def __init__(self, mesh_shape, order, send, recv):
+        self.shape, self.send, self.recv = mesh_shape, send, recv
+        self.place = {name: axis for axis, name in enumerate(order)}
+        self.order = order
+        self.y, self.x, self.has = neighbours(mesh_shape)
+        self.copies = []
+
+    def target(self, direction):
+        y, x = device(direction, self.y, self.x, self.shape)
+        at = {"gy": y, "gx": x}
+        return tuple(at[name] for name in self.order)
+
+    def barrier(self):
+        barrier = pltpu.get_barrier_semaphore()
+        count = 0
+        for direction, there in self.has.items():
+            count = count + there.astype(jnp.int32)
+
+            @pl.when(there)
+            def _():
+                pl.semaphore_signal(barrier, inc=1, device_id=self.target(direction), device_id_type=MESH)
+
+        pl.semaphore_wait(barrier, count)
+
+    def copy(self, direction, source, target, also=None):
+        n = len(self.copies)
+        descriptor = pltpu.make_async_remote_copy(
+            src_ref=source, dst_ref=target, send_sem=self.send.at[n], recv_sem=self.recv.at[n],
+            device_id=self.target(direction), device_id_type=MESH,
+        )
+        both = (lambda p: p) if also is None else (lambda p: p & self.has[also])
+        self.copies.append((descriptor, both(self.has[direction]), both(self.has[OPPOSITE[direction]])))
+        return n
+
+    def start(self, n):
+        descriptor, sends, _ = self.copies[n]
+        pl.when(sends)(descriptor.start)
+
+    def arrived(self, n, then=None):
+        descriptor, _, receives = self.copies[n]
+
+        @pl.when(receives)
+        def _():
+            descriptor.wait_recv()
+            if then is not None:
+                then()
+
+    def finish(self):
+        for descriptor, sends, _ in self.copies:
+            pl.when(sends)(descriptor.wait_send)
+
+
+def halo_kernel(mesh_shape, order, field, measured, perm, above, below, before, after, root, values, send, recv, sem):
+    tile = field.shape[1]
+    slots = measured.shape[0]
+    loads = [
+        pltpu.make_async_copy(measured.at[:, :, pl.ds(i * LANES, LANES)], values.at[:, i], sem.at[i]) for i in range(2)
+    ]
+    for load in loads:
+        load.start()
+    net = Exchange(mesh_shape, order, send, recv)
+    low, mid, high = pl.ds(0, HALO), pl.ds(HALO, tile - 2 * HALO), pl.ds(tile - HALO, HALO)
+    rows = {"up": (low, below), "down": (high, above)}
+    vertical = {
+        (direction, i): net.copy(direction, field.at[:, part, columns], target.at[:, :, columns])
+        for i, columns in enumerate((low, high, mid))
+        for direction, (part, target) in rows.items()
+    }
+    inside = pl.ds(HALO, tile)
+    sides = [
+        net.copy("left", field.at[:, :, low], after.at[:, inside, :]),
+        net.copy("right", field.at[:, :, high], before.at[:, inside, :]),
+    ]
+    corners = []
+    for source, also, place, direction in (
+        (above, "up", pl.ds(0, HALO), "down"),
+        (below, "down", pl.ds(HALO + tile, HALO), "up"),
+    ):
+        corners.append((direction, 0, net.copy("left", source.at[:, :, low], after.at[:, place, :], also)))
+        corners.append((direction, 1, net.copy("right", source.at[:, :, high], before.at[:, place, :], also)))
+
+    net.barrier()
+    for i in (0, 1):
+        for direction in rows:
+            net.start(vertical[direction, i])
+    for n in sides:
+        net.start(n)
+    for direction in rows:
+        net.start(vertical[direction, 2])
+
+    for load in loads:
+        load.wait()
+
+    @pl.loop(0, slots)
+    def _(slot):
+        for half in range(2):
+            x = jnp.sqrt(jnp.concatenate([values[slot, i, pl.ds(half, H, stride=2), :] for i in range(2)], axis=1))
+            first = x.astype(BF16)
+            x = x - first.astype(F32)
+            second = x.astype(BF16)
+            third = (x - second.astype(F32)).astype(BF16)
+            root[slot, half * H:(half + 1) * H, :] = dot(first, perm[...]) + dot(second, perm[...]) + dot(third, perm[...])
+
+    for direction, i, n in corners:
+        net.arrived(vertical[direction, i], lambda: net.start(n))
+    for n in sides:
+        net.arrived(n)
+    for direction in rows:
+        net.arrived(vertical[direction, 2])
+    for _, _, n in corners:
+        net.arrived(n)
+    net.finish()
+
+
+def halo_call(mesh_shape, order, field, measured):
+    tile = field.shape[1]
+    side = tile + 2 * HALO
+    perm = np.zeros((W, W), np.float32)
+    for k in range(W):
+        perm[k, (k % 2) * H + k // 2] = 1.0
+    hbm = pl.BlockSpec(memory_space=pl.ANY)
+    vmem = pl.BlockSpec(memory_space=pltpu.VMEM)
+    strip = jax.ShapeDtypeStruct((2, HALO, tile), F32)
+    column = jax.ShapeDtypeStruct((2, side, HALO), F32)
+    return pl.pallas_call(
+        functools.partial(halo_kernel, mesh_shape, order),
+        out_shape=(strip, strip, column, column, jax.ShapeDtypeStruct(measured.shape, F32)),
+        in_specs=[hbm, hbm, vmem],
+        out_specs=(hbm, hbm, hbm, hbm, vmem),
+        scratch_shapes=[
+            pltpu.VMEM((measured.shape[0], 2, W, LANES), F32),
+            pltpu.SemaphoreType.DMA((12,)),
+            pltpu.SemaphoreType.DMA((12,)),
+            pltpu.SemaphoreType.DMA((2,)),
+        ],
+        compiler_params=pltpu.CompilerParams(collective_id=0, has_side_effects=True),
+        name="halo",
+    )(field, measured, jnp.asarray(perm.astype(ml_dtypes.bfloat16)))
+
+
+def sum_kernel(mesh_shape, order, total, out, own, from_left, from_right, from_up, from_down, send, recv, sem):
+    blocks = own.shape[1]
+    side = own.shape[2]
+    tile = side - 2 * HALO
+    loads = [
+        pltpu.make_async_copy(total.at[:, 1 + i], own.at[:, i], sem.at[i]) for i in range(blocks)
+    ]
+    for load in loads:
+        load.start()
+    net = Exchange(mesh_shape, order, send, recv)
+    low, mid, high = pl.ds(0, HALO), pl.ds(HALO, tile), pl.ds(HALO + tile, HALO)
+    across = {
+        (direction, i): net.copy(direction, total.at[:, block, rows, :], target.at[:, rows, :])
+        for i, rows in enumerate((low, high, mid))
+        for direction, block, target in (("left", 0, from_right), ("right", blocks + 1, from_left))
+    }
+    vertical = {}
+    for direction, rows, target in (("up", low, from_down), ("down", high, from_up)):
+        centre = pl.ds(1, blocks - 2)
+        vertical[direction, 2] = net.copy(direction, total.at[:, pl.ds(2, blocks - 2), rows, :], target.at[:, centre])
+        for i, block in ((0, 0), (1, blocks - 1)):
+            vertical[direction, i] = net.copy(direction, own.at[:, block, rows, :], target.at[:, block])
+
+    net.barrier()
+    for i in (0, 1):
+        for direction in ("left", "right"):
+            net.start(across[direction, i])
+    for direction in ("up", "down"):
+        net.start(vertical[direction, 2])
+    for direction in ("left", "right"):
+        net.start(across[direction, 2])
+    for load in loads:
+        load.wait()
+
+    def add(block, rows, source):
+        def then():
+            own[:, block, rows, :] = own[:, block, rows, :] + source[:, rows, :]
+        return then
+
+    for i, rows, direction in ((0, low, "up"), (1, high, "down")):
+        net.arrived(across["right", i], add(0, rows, from_left))
+        net.start(vertical[direction, 0])
+        net.arrived(across["left", i], add(blocks - 1, rows, from_right))
+        net.start(vertical[direction, 1])
+    net.arrived(across["right", 2], add(0, mid, from_left))
+    net.arrived(across["left", 2], add(blocks - 1, mid, from_right))
+
+    def add_rows(block, count, rows, source):
+        def then():
+            for i in range(block, block + count):
+                own[:, i, rows, :] = own[:, i, rows, :] + source[:, i]
+        return then
+
+    first, last = pl.ds(HALO, HALO), pl.ds(tile, HALO)
+    for i, block, count in ((2, 1, blocks - 2), (0, 0, 1), (1, blocks - 1, 1)):
+        net.arrived(vertical["down", i], add_rows(block, count, first, from_up))
+        net.arrived(vertical["up", i], add_rows(block, count, last, from_down))
+    stores = [
+        pltpu.make_async_copy(own.at[:, i, mid, :], out.at[:, :, pl.ds(i * LANES, LANES)], sem.at[i]) for i in range(blocks)
+    ]
+    for store in stores:
+        store.start()
+    for store in stores:
+        store.wait()
+    net.finish()
+
+
+def sum_call(mesh_shape, order, total):
+    side = total.shape[2]
+    tile = side - 2 * HALO
+    blocks = tile // LANES
+    hbm = pl.BlockSpec(memory_space=pl.ANY)
+    return pl.pallas_call(
+        functools.partial(sum_kernel, mesh_shape, order),
+        out_shape=jax.ShapeDtypeStruct((2, tile, tile), F32),
+        in_specs=[hbm],
+        out_specs=hbm,
+        scratch_shapes=[
+            pltpu.VMEM((2, blocks, side, LANES), F32),
+            pltpu.VMEM((2, side, LANES), F32),
+            pltpu.VMEM((2, side, LANES), F32),
+            pltpu.VMEM((2, blocks, HALO, LANES), F32),
+            pltpu.VMEM((2, blocks, HALO, LANES), F32),
+            pltpu.SemaphoreType.DMA((12,)),
+            pltpu.SemaphoreType.DMA((12,)),
+            pltpu.SemaphoreType.DMA((blocks,)),
+        ],
+        compiler_params=pltpu.CompilerParams(collective_id=1, has_side_effects=True),
+        name="sums",
+    )(total)
+
+
 def frames_kernel(
-    spots, count, tables, probe, root, own, above, below, before, after,
+    mesh_shape, spots, count, tables, probe, root, own, above, below, before, after,
     total_out,
     ext, total, patch, stage2, wave, stage3, stage4, grad, sem,
 ):
     modes = probe.shape[0]
     tile = own.shape[1]
     side = tile + 2 * HALO
-    copies = []
-
-    def load(source, rows, first):
+    blocks = tile // LANES
+    _, _, has = neighbours(mesh_shape)
+    n = 0
+    waits = []
+
+    def load(there, source, block, start, rows):
+        nonlocal n
+        copies = []
         for i in range(source.shape[2] // LANES):
-            n = len(copies)
-            copy = pltpu.make_async_copy(source.at[:, :, pl.ds(i * LANES, LANES)], ext.at[:, first + i, rows, :], sem.at[n])
-            copy.start()
-            copies.append(copy)
-
-    load(own, pl.ds(HALO, tile), 1)
-    load(above, pl.ds(0, HALO), 1)
-    load(below, pl.ds(HALO + tile, HALO), 1)
-    load(before, pl.ds(0, side), 0)
-    load(after, pl.ds(0, side), 1 + tile // LANES)
+            copies.append(pltpu.make_async_copy(
+                source.at[:, pl.ds(start if source.shape[1] == side else 0, rows), pl.ds(i * LANES, LANES)],
+                ext.at[:, block + i, pl.ds(start, rows), :], sem.at[n]))
+            n += 1
+
+        @pl.when(there)
+        def _():
+            for copy in copies:
+                copy.start()
+
+        @pl.when(jnp.logical_not(there))
+        def _():
+            for i in range(len(copies)):
+                for part in range(2):
+                    ext[part, block + i, start:start + rows, :] = jnp.zeros((rows, LANES), F32)
+
+        waits.append((there, copies))
+
+    load(jnp.asarray(True), own, 1, HALO, tile)
+    load(has["up"], above, 1, 0, HALO)
+    load(has["down"], below, 1, HALO + tile, HALO)
+    for name, source, block in (("left", before, 0), ("right", after, 1 + blocks)):
+        load(has[name], source, block, HALO, tile)
+        load(has[name] & has["up"], source, block, 0, HALO)
+        load(has[name] & has["down"], source, block, HALO + tile, HALO)
 
     @pl.loop(0, side // 16)
     def _(i):
         total[:, :, pl.ds(pl.multiple_of(i * 16, 16), 16), :] = jnp.zeros((2, total.shape[1], 16, LANES), F32)
 
-    for copy in copies:
-        copy.wait()
+    for there, copies in waits:
+        @pl.when(there)
+        def _():
+            for copy in copies:
+                copy.wait()
 
     lane = lax.broadcasted_iota(jnp.int32, (W, LANES), 1)
 
@@ -163,7 +439,7 @@
                 total[where] = total[where] + piece
 
     copies = [
-        pltpu.make_async_copy(total.at[:, i], total_out.at[:, :, pl.ds(i * LANES, LANES)], sem.at[i])
+        pltpu.make_async_copy(total.at[:, i], total_out.at[:, i], sem.at[i])
         for i in range(side // LANES)
     ]
     for copy in copies:
@@ -172,7 +448,7 @@
         copy.wait()
 
 
-def frames_call(spots, count, probe, root, own, above, below, before, after):
+def frames_call(mesh_shape, spots, count, probe, root, own, above, below, before, after):
     modes = probe.shape[0]
     side = own.shape[1] + 2 * HALO
     wide = side + LANES
@@ -180,8 +456,8 @@
     vmem = pl.BlockSpec(memory_space=pltpu.VMEM)
     hbm = pl.BlockSpec(memory_space=pl.ANY)
     return pl.pallas_call(
-        frames_kernel,
-        out_shape=jax.ShapeDtypeStruct((2, side, side), F32),
+        functools.partial(frames_kernel, mesh_shape),
+        out_shape=jax.ShapeDtypeStruct((2, side // LANES, side, LANES), F32),
         in_specs=[smem, smem, vmem, vmem, vmem, hbm, hbm, hbm, hbm, hbm],
         out_specs=hbm,
         scratch_shapes=[
@@ -193,55 +469,23 @@
             pltpu.VMEM((modes, 2, W, W), BF16),
             pltpu.VMEM((2, modes, W, W), BF16),
             pltpu.VMEM((2, W, W), F32),
-            pltpu.SemaphoreType.DMA((16,)),
+            pltpu.SemaphoreType.DMA((32,)),
         ],
         compiler_params=pltpu.CompilerParams(vmem_limit_bytes=60 * 1024 * 1024),
         name="frames",
     )(spots, count, jnp.asarray(dft_tables()), probe, root, own, above, below, before, after)
 
 
-def passed_along(array, axis, by):
-    devices = lax.axis_size(axis)
-    pairs = [(i, i + by) for i in range(devices) if 0 <= i + by < devices]
-    return lax.ppermute(array, axis, pairs)
-
-
-def body(object_field, probe, positions, frame_count, measured):
-    border = HALO
-    spots = positions[0, 0]
-    count = frame_count
-    root = jnp.sqrt(measured[0, 0])
-    slots = root.shape[0]
-    root = root.reshape(slots, H, 2, H, 2).transpose(0, 2, 1, 4, 3).reshape(slots, W, W)
-    above = passed_along(object_field[:, -border:, :], "gy", 1)
-    below = passed_along(object_field[:, :border, :], "gy", -1)
-    left = jnp.concatenate([x[:, :, :border] for x in (above, object_field, below)], axis=1)
-    right = jnp.concatenate([x[:, :, -border:] for x in (above, object_field, below)], axis=1)
-    before = passed_along(right, "gx", 1)
-    after = passed_along(left, "gx", -1)
-
-    total = frames_call(spots, count, probe, root, object_field, above, below, before, after)
-
-    upper_rim = total[:, :border, :]
-    lower_rim = total[:, -border:, :]
-    from_below = passed_along(upper_rim, "gy", -1)
-    from_above = passed_along(lower_rim, "gy", 1)
-    middle = total[:, border:-border, :]
-    middle = middle.at[:, -border:, :].add(from_below)
-    middle = middle.at[:, :border, :].add(from_above)
-    left_rim = middle[:, :, :border]
-    right_rim = middle[:, :, -border:]
-    from_right = passed_along(left_rim, "gx", -1)
-    from_left = passed_along(right_rim, "gx", 1)
-    inner = middle[:, :, border:-border]
-    inner = inner.at[:, :, -border:].add(from_right)
-    inner = inner.at[:, :, :border].add(from_left)
-    return inner
+def body(mesh_shape, order, object_field, probe, positions, frame_count, measured):
+    above, below, before, after, root = halo_call(mesh_shape, order, object_field, measured[0, 0])
+    total = frames_call(mesh_shape, positions[0, 0], frame_count, probe, root, object_field, above, below, before, after)
+    return sum_call(mesh_shape, order, total)
 
 
 def solution(mesh):
+    mesh_shape = (mesh.shape["gy"], mesh.shape["gx"])
     return jax.shard_map(
-        body,
+        functools.partial(body, mesh_shape, tuple(mesh.axis_names)),
         mesh=mesh,
         in_specs=(
             P(None, "gy", "gx"),

time: 164 us -> 74.5 us (0.45)
  the two profiles are of different devices: /device:TPU:24 before, /device:TPU:8 now
where the time goes in v2:
time: 74.5 us; the launch traced here: 73 us
  Pallas kernels  67.9 us (91%)
  local copies, waits for them, and re-layouts  4.42 us (6%)
    pallas_call x1, Pallas kernels, halo_call(): pl.pallas_call(functools.partial(halo_kernel, mesh_shape, order), out_sha...  27.5 us
    pallas_call x1, Pallas kernels, sum_call(): pl.pallas_call(functools.partial(sum_kernel, mesh_shape, order), out_shap...  25.6 us
    pallas_call x1, Pallas kernels, frames_call(): pl.pallas_call(functools.partial(frames_kernel, mesh_shape), out_shape=ja...  14.8 us
    unnamed x1, local copies, waits for them, and re-layouts  3.08 us

profile of v2, /device:TPU:8, one launch (start us, length us, event | category | flops | bytes accessed | tf_op | source)
XLA Modules:
  0.0 73.0 jit_solution(11094522091649848246)
XLA Ops:
  0.7 1.3 %copy.8.spots = s32[4,2]{1,0:T(4,128)} copy(s32[4,2]{0,1:T(2,128)} %bitcast.3) | data formatting | bytes 64 | tf_op jit(solution)/shard_map/squeeze | solution.py:481
  2.0 27.5 %halo.1 = (f32[2,128,512]{2,1,0:T(8,128)}, f32[2,128,512]{2,1,0:T(8,128)}, f32[2,768,128]{2,1,0:T(8,128)}, f32[2,768,128]{2,1,0:T(8,128)}, f32[4,256,256]{2,1,0:T(8,128)}) custom-call(f32[2,512,512]{2,1,0:T(8,128)} %own.1, f32[4,256,256]{2,1,0:T(8,128)} %bitcast.2, bf16[256,256]{1,0:T(8,128)(2,1)} %constant.4.clone.perm), custom_call_target="tpu_custom_call" | custom-call | tf_op jit(solution)/shard_map/halo/pallas_call | solution.py:183
  29.5 14.8 %frames.1.total = f32[2,6,768,128]{3,2,1,0:T(8,128)} custom-call(s32[4,2]{1,0:T(4,128)} %copy.8.spots, s32[1,1]{1,0:T(1,128)S(6)} %copy.10.count, bf16[4,256,256]{2,1,0:T(8,128)(2,1)} %constant.5.clone.tables, f32[3,2,256,256]{3,2,1,0:T(8,128)} %probe.1, f32[4,256,256]{2,1,0:T(8,128)} %get-tuple-element.10.root, f32[2,512,512]{2,1,0:T(8,128)} %own.1, ...), custom_call_target="tpu_custom_call" | custom-call | tf_op jit(solution)/shard_map/frames/pallas_call | solution.py:458
  44.3 25.6 %sums.1 = f32[2,512,512]{2,1,0:T(8,128)} custom-call(f32[2,6,768,128]{3,2,1,0:T(8,128)} %frames.1.total), custom_call_target="tpu_custom_call" | custom-call | tf_op jit(solution)/shard_map/sums/pallas_call | solution.py:271
  69.9 3.1 %copy.11 = f32[2,512,512]{2,1,0:T(8,128)} copy(f32[2,512,512]{2,1,0:T(8,128)} %sums.1) | data formatting | bytes 4194304
